TPU v7x, 32 devices: a whole 2x2x4 slice. The times are simulated.
32 devices in a mesh: groups: 2 (over y), rows: 4 (over z), blocks: 2 (over x), cols: 2 (over core).
Axes of the slice: x: 2, y: 2, z: 4, core: 2. Of those that a mesh axis runs over, the one named last changes fastest.
Arguments:
- inputs: bfloat16 [4096, 1024], P(('groups', 'rows')), parts along dimension 0, may hold values from -6 to 6
- projection: bfloat16 [1024, 8192], P(None, ('groups', 'blocks', 'cols')), parts along dimension 1, may hold values from -0.1875 to 0.1875
- phases: bfloat16 [8192], P(('groups', 'blocks', 'cols')), parts along dimension 0, may hold values from -3.140625 to 3.140625
- inverse_blocks: float32 [4, 2048, 2048], P(('groups', 'blocks'), 'rows'), parts along dimension 0, as said below
- labels: int32 [4096], P(('groups', 'rows')), parts along dimension 0, may hold values from 0 to 999
- predictions: float32 [4096, 1000], P(('groups', 'rows'), 'cols'), parts along dimension 0, may hold values from -4 to 4
- coefficients: float32 [8192, 1000], P(('groups', 'blocks', 'rows'), 'cols'), parts along dimension 0, may hold values from -3 to 3
Outputs:
- new_coefficients: float32 [8192, 1000], P(('groups', 'blocks', 'rows'), 'cols'), parts along dimension 0
- new_predictions: float32 [4096, 1000], P(('groups', 'rows'), 'cols'), parts along dimension 0
There are 2 independent parts, one for each index of `groups`. A program takes and returns all parts, laid end to end along the dimension named above; each array names one. Nothing has to cross between parts.
Inputs may be any that keep to these rules, and one draw needn't show every extreme that they name: `inverse_blocks`: one dense preconditioner for each feature block.
All inputs are finite; a program needn't handle non-finite values.
Results may differ from a plain program's by a relative error of at most 0.0029.
Values may be sent and summed in bfloat16 or wider, within the bound.
No kernel may reach another device: no remote copies, remote signals or barrier semaphores. Data moves between devices by JAX's collectives and lax.ppermute only.
A program may use at most 64 MiB of HBM per device.

v0:
```python
import jax
import jax.numpy as jnp
from jax import lax
from jax.sharding import PartitionSpec as P

DAMPING = 0.5


def cosine_features(inputs, projection, phases):
    angles = (
        jnp.dot(inputs, projection, preferred_element_type=jnp.float32)
        + phases.astype(jnp.float32)[None, :]
    )
    return jnp.cos(angles).astype(jnp.bfloat16)


def shards(inputs, projection, phases, inverse_blocks, labels, predictions, coefficients):
    out_width = predictions.shape[1]
    classes = lax.axis_index("cols") * out_width + jnp.arange(out_width, dtype=jnp.int32)
    onehot = (labels[:, None] == classes[None, :]).astype(jnp.float32)
    residual = (onehot - predictions).astype(jnp.bfloat16)
    half_features = cosine_features(inputs, projection, phases)
    features_full = lax.all_gather(half_features, "cols", axis=1, tiled=True)
    local_inverse = inverse_blocks[0]
    column_slice = features_full
    own_gradient = lax.psum_scatter(
        lax.dot_general(
            column_slice, residual, (((0,), (0,)), ((), ())), preferred_element_type=jnp.float32
        ),
        "rows",
        scatter_dimension=0,
        tiled=True,
    )
    gradient = lax.all_gather(own_gradient, "rows", axis=0, tiled=True)
    solved = jnp.dot(local_inverse, gradient, precision=lax.Precision.HIGHEST)
    step_update = DAMPING * solved
    new_coefficients = coefficients + step_update
    column_slice = features_full
    contribution = jnp.dot(
        column_slice,
        lax.all_gather(step_update.astype(jnp.bfloat16), "rows", axis=0, tiled=True),
        preferred_element_type=jnp.float32,
    )
    summed = lax.psum(contribution, "blocks")
    return (new_coefficients, predictions + summed)


def solution(mesh):
    return jax.shard_map(
        shards,
        mesh=mesh,
        in_specs=(
            P(("groups", "rows"), None),
            P(None, ("groups", "blocks", "cols")),
            P(("groups", "blocks", "cols")),
            P(("groups", "blocks"), "rows", None),
            P(("groups", "rows")),
            P(("groups", "rows"), "cols"),
            P(("groups", "blocks", "rows"), "cols"),
        ),
        out_specs=(P(("groups", "blocks", "rows"), "cols"), P(("groups", "rows"), "cols")),
        check_vma=False,
    )
```

profile of v0, /device:TPU:0, one launch (start us, length us, event | category | flops | bytes accessed | tf_op | source)
XLA Modules:
  0.0 311.2 jit_solution(1773116370345842166)
XLA Ops:
  7.2 0.0 copy-start
  7.2 0.0 all-gather.4.cloned.1.call-start
  7.2 0.8 convert_element_type.15
  8.0 0.7 copy-done
  8.8 0.0 copy-start.1
  8.8 0.0 copy-start.2
  8.8 9.8 %cosine_convert_fusion = bf16[512,1024]{1,0:T(8,128)(2,1)} fusion(bf16[512,1024]{1,0:T(8,128)(2,1)} %param.7, bf16[1024,1024]{1,0:T(8,128)(2,1)S(1)} %copy-done, f32[1024]{0:T(1024)S(1)} %convert_element_type.15), kind=kOutput, calls=%fused_computation.2 | convolution fusion | flops 1074790400 | bytes 4198400 | tf_op jit(solution)/shard_map/dot_general | solution.py:11
  18.6 0.0 all-gather.4.cloned.1.call-update
  18.6 0.0 reduce-scatter.2.cloned.1.call-start
  18.7 13.4 %all-gather.4.cloned.1.call-done = bf16[512,2048]{1,0:T(8,128)(2,1)} async-done(((bf16[512,1024]{1,0:T(8,128)(2,1)}), bf16[512,2048]{1,0:T(8,128)(2,1)}) %all-gather.4.cloned.1.call-update) | async-done | bytes 2097168 | tf_op jit(solution)/shard_map/all_gather | solution.py:23
  32.1 0.0 copy-done.1
  32.1 0.0 copy-done.2
  32.1 5.0 %fusion.8 = f32[2048,500]{1,0:T(8,128)} fusion(bf16[512,2048]{1,0:T(8,128)(2,1)} %all-gather.4.cloned.1.call-done, f32[512,500]{0,1:T(8,128)S(1)} %copy-done.1, s32[512]{0:T(512)S(1)} %copy-done.2, s32[500]{0:T(512)S(1)} %iota_add_fusion), kind=kOutput, calls=%fused_computation.6 | convolution fusion | flops 1049600000 | bytes 7221200 | tf_op jit(solution)/shard_map/dot_general | solution.py:27
  37.0 0.0 reduce-scatter.2.cloned.1.call-update
  37.0 0.0 all-gather.6.cloned.1.call-start
  37.1 78.0 %reduce-scatter.2.cloned.1.call-done = f32[512,500]{1,0:T(8,128)} async-done(((f32[2048,500]{1,0:T(8,128)}), f32[512,500]{1,0:T(8,128)}) %reduce-scatter.2.cloned.1.call-update) | async-done | bytes 1024016 | tf_op jit(solution)/shard_map/reduce_scatter | solution.py:26
  115.1 0.0 all-gather.6.cloned.1.call-update
  115.2 0.2 all-gather.8.cloned.1.call-start
  115.4 82.7 %all-gather.6.cloned.1.call-done = f32[2048,500]{1,0:T(8,128)} async-done(((f32[512,500]{1,0:T(8,128)}), f32[2048,500]{1,0:T(8,128)}) %all-gather.6.cloned.1.call-update) | async-done | bytes 4096016 | tf_op jit(solution)/shard_map/all_gather | solution.py:34
  198.1 17.2 %fusion.11 = (bf16[512,500]{0,1:T(8,128)(2,1)}, f32[512,500]{0,1:T(8,128)}) fusion(f32[512,500]{0,1:T(8,128)} %param.13, f32[2048,500]{1,0:T(8,128)} %all-gather.6.cloned.1.call-done, f32[1,512,2048]{2,1,0:T(8,128)} %param.10), kind=kOutput, calls=%fused_computation.10 | convolution fusion | flops 6292224000 | bytes 10850304 | tf_op jit(solution)/shard_map/dot_general | solution.py:35
  215.3 0.0 all-gather.8.cloned.1.call-update
  215.3 0.0 all-reduce.2.cloned.1.call-start
  215.4 43.9 %all-gather.8.cloned.1.call-done = bf16[2048,500]{0,1:T(8,128)(2,1)} async-done(((bf16[512,500]{0,1:T(8,128)(2,1)}), bf16[2048,500]{0,1:T(8,128)(2,1)}) %all-gather.8.cloned.1.call-update) | async-done | bytes 2048016 | tf_op jit(solution)/shard_map/all_gather | solution.py:41
  259.3 4.4 %fusion.12 = f32[512,500]{0,1:T(8,128)} fusion(bf16[512,2048]{1,0:T(8,128)(2,1)} %all-gather.4.cloned.1.call-done, bf16[2048,500]{0,1:T(8,128)(2,1)} %all-gather.8.cloned.1.call-done), kind=kOutput, calls=%fused_computation.11 | convolution fusion | flops 1048576000 | bytes 5169152 | tf_op jit(solution)/shard_map/dot_general | solution.py:39
  263.7 0.0 all-reduce.2.cloned.1.call-update
  263.8 38.6 %all-reduce.2.cloned.1.call-done = f32[512,500]{0,1:T(8,128)} async-done(((f32[512,500]{0,1:T(8,128)}), f32[512,500]{0,1:T(8,128)}) %all-reduce.2.cloned.1.call-update) | async-done | bytes 1024016 | tf_op jit(solution)/shard_map/psum | solution.py:44
  302.3 2.4 add.33
  (1 shorter events, 0.0 us)
Async XLA Ops:
  7.2 1.6 copy-start
  7.2 24.9 %all-gather.4.cloned.1.call-start = ((), (), s32[]{:S(2)}) async-start(), calls=%async_computation.1 | async-start | bytes 3145728 | tf_op jit(solution)/shard_map/all_gather | solution.py:23
  8.8 23.3 %copy-start.1 = (f32[512,500]{0,1:T(8,128)S(1)}, f32[512,500]{0,1:T(8,128)}, u32[]{:S(2)}) copy-start(f32[512,500]{0,1:T(8,128)} %param.12) | copy-start | bytes 3072004
  8.8 23.3 %copy-start.2 = (s32[512]{0:T(512)S(1)}, s32[512]{0:T(512)}, u32[]{:S(2)}) copy-start(s32[512]{0:T(512)} %param.11) | copy-start | bytes 6148
  18.6 96.5 %reduce-scatter.2.cloned.1.call-start = ((), (), s32[]{:S(2)}) async-start(), calls=%async_computation.2 | async-start | bytes 5242880 | tf_op jit(solution)/shard_map/reduce_scatter | solution.py:26
  37.0 161.1 %all-gather.6.cloned.1.call-start = ((), (), s32[]{:S(2)}) async-start(), calls=%async_computation.3 | async-start | bytes 5242880 | tf_op jit(solution)/shard_map/all_gather | solution.py:34
  115.2 144.1 %all-gather.8.cloned.1.call-start = ((), (), s32[]{:S(2)}) async-start(), calls=%async_computation.4 | async-start | bytes 2580480 | tf_op jit(solution)/shard_map/all_gather | solution.py:41
  215.3 87.0 %all-reduce.2.cloned.1.call-start = ((), (), s32[]{:S(2)}) async-start(), calls=%async_computation.5 | async-start | bytes 2064384 | tf_op jit(solution)/shard_map/psum | solution.py:44
Sparse Core Ops, SparseCore 0:
  18.7 13.2 all-gather.3
  37.2 77.9 reduce-scatter.1
  116.8 81.2 all-gather.5
  215.4 43.8 all-gather.7
  263.9 38.3 all-reduce.1
where the time goes:
time: 311 us
  waiting for transfers between devices  257 us (83%)
  matrix products  36.4 us (12%)
  between operations  13.8 us (4%)
  other arithmetic  3.21 us (1%)
    all_gather x1, waiting for transfers between devices, shards(): gradient = lax.all_gather(own_gradient, 'rows', axis=0, tiled=True)  82.7 us
    reduce_scatter x1, waiting for transfers between devices, shards(): lax.psum_scatter(lax.dot_general(column_slice, residual, (((0,), (0,)), (...  78 us
    all_gather x1, waiting for transfers between devices, shards(): lax.all_gather(step_update.astype(jnp.bfloat16), 'rows', axis=0, tiled=True)  43.9 us
    psum x1, waiting for transfers between devices, shards(): summed = lax.psum(contribution, 'blocks')  38.6 us
    dot_general x1, matrix products, shards(): solved = jnp.dot(local_inverse, gradient, precision=lax.Precision.HIGHEST)  17.2 us
    all_gather x1, waiting for transfers between devices, shards(): features_full = lax.all_gather(half_features, 'cols', axis=1, tiled=True)  13.4 us
    dot_general x1, matrix products, cosine_features(): jnp.dot(inputs, projection, preferred_element_type=jnp.float32)  9.81 us
  transfers between devices with their start and end apart: 5, of which 5 were waited for; matrix products, arithmetic and copies ran while one was open for 0% of the time, Pallas kernels for 0%

commit v1 on v0

--- a/solution.py
+++ b/solution.py
@@ -4,6 +4,28 @@
 from jax.sharding import PartitionSpec as P
 
 DAMPING = 0.5
+
+
+def laid_out(blocks, dim):
+    blocks = jnp.moveaxis(blocks, 0, dim)
+    lengths = blocks.shape
+    return blocks.reshape(*lengths[:dim], lengths[dim] * lengths[dim + 1], *lengths[dim + 2 :])
+
+
+def gather_around(shard, axis, dim):
+    count = lax.axis_size(axis)
+    pairs = [(i, (i + 1) % count) for i in range(count)]
+    back = [(b, a) for a, b in pairs]
+    lower, upper = ([], [])
+    for step in range(count - 1):
+        if step % 2 == 0:
+            lower.append(lax.ppermute(lower[-1] if lower else shard, axis, pairs))
+        else:
+            upper.append(lax.ppermute(upper[-1] if upper else shard, axis, back))
+    blocks = jnp.stack([*lower[::-1], shard, *upper])
+    shift = lax.axis_index(axis) - len(lower)
+    blocks = blocks[(jnp.arange(count) - shift) % count]
+    return laid_out(blocks, dim)
 
 
 def cosine_features(inputs, projection, phases):
@@ -31,7 +53,7 @@
         scatter_dimension=0,
         tiled=True,
     )
-    gradient = lax.all_gather(own_gradient, "rows", axis=0, tiled=True)
+    gradient = gather_around(own_gradient, "rows", 0)
     solved = jnp.dot(local_inverse, gradient, precision=lax.Precision.HIGHEST)
     step_update = DAMPING * solved
     new_coefficients = coefficients + step_update

time: 311 us -> 314 us (level)
  waiting for transfers between devices: 257 us -> 221 us
  starting transfers between devices: 0.38 us -> 23.7 us
  local copies, waits for them, and re-layouts: 0.74 us -> 10.9 us
  other arithmetic: 3.21 us -> 7.82 us
    all_gather x1 -> x0, waiting for transfers between devices: 82.7 us -> none  [shards(): gradient = lax.all_gather(own_gradient, 'rows', axis=0, tiled=True)]
    ppermute x0 -> x3, waiting for transfers between devices: none -> 47.3 us  [the longest x2 45.5 us: gather_around(): lower.append(lax.ppermute(lower[-1] if lower else shard, axis, pairs))]
    ppermute x0 -> x3, starting transfers between devices: none -> 23.6 us  [the longest x2 21.2 us: gather_around(): lower.append(lax.ppermute(lower[-1] if lower else shard, axis, pairs))]
    gather x0 -> x2, local copies, waits for them, and re-layouts: none -> 10.2 us  [gather_around(): blocks = blocks[(jnp.arange(count) - shift) % count]]
    another operation x0 -> x1, other arithmetic: none -> 4.59 us  [gather_around(): blocks = jnp.stack([*lower[::-1], shard, *upper])]
  transfers between devices with their start and end apart: 5 -> 7, of which waited for: 5 -> 7; matrix products, arithmetic and copies ran while one was open for 0% -> 0% of each run, Pallas kernels for 0% -> 0%
where the time goes in v1:
time: 314 us; the launch traced here: 313 us
  waiting for transfers between devices  221 us (70%)
  matrix products  36.2 us (12%)
  starting transfers between devices  23.7 us (8%)
  between operations  13.8 us (4%)
  local copies, waits for them, and re-layouts  10.9 us (3%)
  other arithmetic  7.82 us (2%)
    reduce_scatter x1, waiting for transfers between devices, shards(): lax.psum_scatter(lax.dot_general(column_slice, residual, (((0,), (0,)), (...  77 us
    ppermute x2, waiting for transfers between devices, gather_around(): lower.append(lax.ppermute(lower[-1] if lower else shard, axis, pairs))  45.5 us
    all_gather x1, waiting for transfers between devices, shards(): lax.all_gather(step_update.astype(jnp.bfloat16), 'rows', axis=0, tiled=True)  44.6 us
    psum x1, waiting for transfers between devices, shards(): summed = lax.psum(contribution, 'blocks')  38.6 us
    ppermute x2, starting transfers between devices, gather_around(): lower.append(lax.ppermute(lower[-1] if lower else shard, axis, pairs))  21.2 us
    dot_general x1, matrix products, shards(): solved = jnp.dot(local_inverse, gradient, precision=lax.Precision.HIGHEST)  17.2 us
    all_gather x1, waiting for transfers between devices, shards(): features_full = lax.all_gather(half_features, 'cols', axis=1, tiled=True)  13.4 us
    gather x2, local copies, waits for them, and re-layouts, gather_around(): blocks = blocks[(jnp.arange(count) - shift) % count]  10.2 us
  transfers between devices with their start and end apart: 7, of which 7 were waited for; matrix products, arithmetic and copies ran while one was open for 0% of the time, Pallas kernels for 0%

profile of v1, /device:TPU:0, one launch (start us, length us, event | category | flops | bytes accessed | tf_op | source)
XLA Modules:
  0.0 313.4 jit_solution(15457695649440282316)
XLA Ops:
  7.2 0.0 copy-start
  7.2 0.0 all-gather.3.cloned.1.call-start
  7.2 0.8 convert_element_type.15
  8.0 0.7 copy-done
  8.8 0.0 copy-start.1
  8.8 0.0 copy-start.2
  8.8 9.8 %cosine_convert_fusion = bf16[512,1024]{1,0:T(8,128)(2,1)} fusion(bf16[512,1024]{1,0:T(8,128)(2,1)} %param.7, bf16[1024,1024]{1,0:T(8,128)(2,1)S(1)} %copy-done, f32[1024]{0:T(1024)S(1)} %convert_element_type.15), kind=kOutput, calls=%fused_computation.4 | convolution fusion | flops 1074790400 | bytes 4198400 | tf_op jit(solution)/shard_map/dot_general | solution.py:33
  18.6 0.0 all-gather.3.cloned.1.call-update
  18.6 0.0 reduce-scatter.2.cloned.1.call-start
  18.7 13.4 %all-gather.3.cloned.1.call-done = bf16[512,2048]{1,0:T(8,128)(2,1)} async-done(((bf16[512,1024]{1,0:T(8,128)(2,1)}), bf16[512,2048]{1,0:T(8,128)(2,1)}) %all-gather.3.cloned.1.call-update) | async-done | bytes 2097168 | tf_op jit(solution)/shard_map/all_gather | solution.py:45
  32.1 0.0 copy-done.1
  32.1 0.0 copy-done.2
  32.1 4.8 %fusion.8 = f32[2048,500]{0,1:T(8,128)} fusion(bf16[512,2048]{1,0:T(8,128)(2,1)} %all-gather.3.cloned.1.call-done, f32[512,500]{0,1:T(8,128)S(1)} %copy-done.1, s32[512]{0:T(512)S(1)} %copy-done.2, s32[500]{0:T(512)S(1)} %iota_add_fusion), kind=kOutput, calls=%fused_computation.8 | convolution fusion | flops 1049600000 | bytes 7221200 | tf_op jit(solution)/shard_map/dot_general | solution.py:49
  36.8 0.0 reduce-scatter.2.cloned.1.call-update
  36.9 0.0 all-gather.5.cloned.1.call-start
  36.9 77.0 %reduce-scatter.2.cloned.1.call-done = f32[512,500]{0,1:T(8,128)} async-done(((f32[2048,500]{0,1:T(8,128)}), f32[512,500]{0,1:T(8,128)}) %reduce-scatter.2.cloned.1.call-update) | async-done | bytes 1024016 | tf_op jit(solution)/shard_map/reduce_scatter | solution.py:48
  113.9 1.4 collective-permute-start
  115.4 2.4 collective-permute-start.2
  117.8 24.0 %collective-permute-done = f32[512,500]{0,1:T(8,128)} collective-permute-done((f32[512,500]{0,1:T(8,128)}, f32[512,500]{0,1:T(8,128)}, u32[]{:S(2)}, u32[]{:S(2)}) %collective-permute-start) | collective-permute-done | bytes 1024032 | tf_op jit(solution)/shard_map/ppermute | solution.py:22
  141.8 19.7 %collective-permute-start.1 = (f32[512,500]{0,1:T(8,128)}, f32[512,500]{0,1:T(8,128)}, u32[]{:S(2)}, u32[]{:S(2)}) collective-permute-start(f32[512,500]{0,1:T(8,128)} %collective-permute-done), channel_id=1, source_target_pairs={{0,4},{4,8},{8,12},{12,0},{1,5},{5,9},{9,13},{13,1},{2,6},{6,10},{... | collective-permute-start | bytes 3072008 | tf_op jit(solution)/shard_map/ppermute | solution.py:22
  161.6 1.8 collective-permute-done.2
  163.3 21.5 %collective-permute-done.1 = f32[512,500]{0,1:T(8,128)} collective-permute-done((f32[512,500]{0,1:T(8,128)}, f32[512,500]{0,1:T(8,128)}, u32[]{:S(2)}, u32[]{:S(2)}) %collective-permute-start.1) | collective-permute-done | bytes 1024032 | tf_op jit(solution)/shard_map/ppermute | solution.py:22
  184.8 4.6 %pad_maximum_fusion = f32[4,512,500]{1,2,0:T(8,128)} fusion(f32[1,512,500]{1,2,0:T(8,128)} %bitcast.3, f32[1,512,500]{1,2,0:T(8,128)} %bitcast.25, f32[1,512,500]{1,2,0:T(8,128)} %bitcast.1, f32[1,512,500]{1,2,0:T(8,128)} %bitcast), kind=kLoop, calls=%fused_computation.3 | loop fusion | flops 3072000 | bytes 8192000 | tf_op jit(solution)/shard_map/stack | solution.py:25
  189.4 4.9 %gather_fusion = f32[4,512,500]{1,2,0:T(8,128)} fusion(f32[4,512,500]{1,2,0:T(8,128)} %pad_maximum_fusion, s32[1024]{0:T(1024)S(1)} %pad_clamp_fusion), kind=kCustom, calls=%fused_computation | custom fusion | bytes 8192016 | tf_op jit(solution)/shard_map/gather | solution.py:27
  194.4 5.2 %copy.9 = f32[4,512,500]{2,1,0:T(8,128)} copy(f32[4,512,500]{1,2,0:T(8,128)} %gather_fusion) | data formatting | bytes 8192000 | tf_op jit(solution)/shard_map/gather | solution.py:27
  199.6 17.2 %fusion.13 = (bf16[512,500]{0,1:T(8,128)(2,1)}, f32[512,500]{0,1:T(8,128)}) fusion(f32[512,500]{0,1:T(8,128)} %param.13, f32[2048,500]{1,0:T(8,128)} %bitcast.24, f32[1,512,2048]{2,1,0:T(8,128)} %param.10), kind=kOutput, calls=%fused_computation.19 | convolution fusion | flops 6292224000 | bytes 10850304 | tf_op jit(solution)/shard_map/dot_general | solution.py:57
  216.8 0.0 all-gather.5.cloned.1.call-update
  216.8 0.0 all-reduce.2.cloned.1.call-start
  216.9 44.6 %all-gather.5.cloned.1.call-done = bf16[2048,500]{0,1:T(8,128)(2,1)} async-done(((bf16[512,500]{0,1:T(8,128)(2,1)}), bf16[2048,500]{0,1:T(8,128)(2,1)}) %all-gather.5.cloned.1.call-update) | async-done | bytes 2048016 | tf_op jit(solution)/shard_map/all_gather | solution.py:63
  261.5 4.4 %fusion.14 = f32[512,500]{0,1:T(8,128)} fusion(bf16[512,2048]{1,0:T(8,128)(2,1)} %all-gather.3.cloned.1.call-done, bf16[2048,500]{0,1:T(8,128)(2,1)} %all-gather.5.cloned.1.call-done), kind=kOutput, calls=%fused_computation.20 | convolution fusion | flops 1048576000 | bytes 5169152 | tf_op jit(solution)/shard_map/dot_general | solution.py:61
  265.9 0.0 all-reduce.2.cloned.1.call-update
  265.9 38.6 %all-reduce.2.cloned.1.call-done = f32[512,500]{0,1:T(8,128)} async-done(((f32[512,500]{0,1:T(8,128)}), f32[512,500]{0,1:T(8,128)}) %all-reduce.2.cloned.1.call-update) | async-done | bytes 1024016 | tf_op jit(solution)/shard_map/psum | solution.py:66
  304.5 2.4 add.59
  (3 shorter events, 0.0 us)
Async XLA Ops:
  7.2 1.6 copy-start
  7.2 24.9 %all-gather.3.cloned.1.call-start = ((), (), s32[]{:S(2)}) async-start(), calls=%async_computation.1 | async-start | bytes 3145728 | tf_op jit(solution)/shard_map/all_gather | solution.py:45
  8.8 23.3 %copy-start.1 = (f32[512,500]{0,1:T(8,128)S(1)}, f32[512,500]{0,1:T(8,128)}, u32[]{:S(2)}) copy-start(f32[512,500]{0,1:T(8,128)} %param.12) | copy-start | bytes 3072004
  8.8 23.3 %copy-start.2 = (s32[512]{0:T(512)S(1)}, s32[512]{0:T(512)}, u32[]{:S(2)}) copy-start(s32[512]{0:T(512)} %param.11) | copy-start | bytes 6148
  18.6 95.3 %reduce-scatter.2.cloned.1.call-start = ((), (), s32[]{:S(2)}) async-start(), calls=%async_computation.2 | async-start | bytes 5160960 | tf_op jit(solution)/shard_map/reduce_scatter | solution.py:48
  36.9 224.6 %all-gather.5.cloned.1.call-start = ((), (), s32[]{:S(2)}) async-start(), calls=%async_computation.3 | async-start | bytes 2580480 | tf_op jit(solution)/shard_map/all_gather | solution.py:63
  113.9 27.9 %collective-permute-start = (f32[512,500]{0,1:T(8,128)}, f32[512,500]{0,1:T(8,128)}, u32[]{:S(2)}, u32[]{:S(2)}) collective-permute-start(f32[512,500]{0,1:T(8,128)} %reduce-scatter.2.cloned.1.call-done), channel_id=1, source_target_pairs={{0,4},{4,8},{8,12},{12,0},{1,5},{5,9},{9,13},{13,1},{2,6},{6,10},{... | collective-permute-start | bytes 3072008 | tf_op jit(solution)/shard_map/ppermute | solution.py:22
  115.4 48.0 %collective-permute-start.2 = (f32[512,500]{0,1:T(8,128)}, f32[512,500]{0,1:T(8,128)}, u32[]{:S(2)}, u32[]{:S(2)}) collective-permute-start(f32[512,500]{0,1:T(8,128)} %reduce-scatter.2.cloned.1.call-done), channel_id=1, source_target_pairs={{4,0},{8,4},{12,8},{0,12},{5,1},{9,5},{13,9},{1,13},{6,2},{10,6},{... | collective-permute-start | bytes 3072008 | tf_op jit(solution)/shard_map/ppermute | solution.py:24
  141.8 43.0 %collective-permute-start.1 = (f32[512,500]{0,1:T(8,128)}, f32[512,500]{0,1:T(8,128)}, u32[]{:S(2)}, u32[]{:S(2)}) collective-permute-start(f32[512,500]{0,1:T(8,128)} %collective-permute-done), channel_id=1, source_target_pairs={{0,4},{4,8},{8,12},{12,0},{1,5},{5,9},{9,13},{13,1},{2,6},{6,10},{... | collective-permute-start | bytes 3072008 | tf_op jit(solution)/shard_map/ppermute | solution.py:22
  216.8 87.7 %all-reduce.2.cloned.1.call-start = ((), (), s32[]{:S(2)}) async-start(), calls=%async_computation.4 | async-start | bytes 2064384 | tf_op jit(solution)/shard_map/psum | solution.py:66
Sparse Core Ops, SparseCore 0:
  18.7 13.2 all-gather.2
  37.0 76.8 reduce-scatter.1
  217.0 44.4 all-gather.4
  266.0 38.3 all-reduce.1
